TPU v7x, 32 devices: a whole 2x2x4 slice. The times are simulated.
32 devices in a mesh: parts: 2 (over y), bank: 8 (over z, x), batch: 2 (over core).
Axes of the slice: x: 2, y: 2, z: 4, core: 2. Of those that a mesh axis runs over, the one named last changes fastest.
Arguments:
- bank: bfloat16 [32768, 256], P(('parts', 'bank')), parts along dimension 0, may hold values from -1 to 1
- queries: bfloat16 [4096, 256], P(('parts', 'batch')), parts along dimension 0, may hold values from -8 to 8
- keys: bfloat16 [4096, 256], P(('parts', 'batch')), parts along dimension 0, may hold values from -0.375 to 0.375
- labels: int32 [4096], P(('parts', 'batch')), parts along dimension 0, may hold values from 0 to 2047, each once
- mask_tiles: int32 [32, 16], P('parts'), parts along dimension 0, may hold values from 0 to 127
Outputs:
- new_bank: bfloat16 [32768, 256], P(('parts', 'bank')), parts along dimension 0
- query_grad: float32 [4096, 256], P(('parts', 'batch')), parts along dimension 0
- loss: float32 [4096], P(('parts', 'batch')), parts along dimension 0
There are 2 independent parts, one for each index of `parts`. A program takes and returns all parts, laid end to end along the dimension named above; each array names one. Nothing has to cross between parts.
Inputs may be any that keep to these rules, and one draw needn't show every extreme that they name: `labels`: a permutation: each row of keys is the positive of exactly one query. `mask_tiles`: tile t holds bank rows t * 128 to t * 128 + 127; row b lists tiles excluded for queries b * 128 to b * 128 + 127; numbers may repeat.
All inputs are finite; a program needn't handle non-finite values.
Results may differ from a plain program's by a relative error of at most 0.0055.
Values may be sent and summed in bfloat16 or wider, within the bound.
A program may use at most 64 MiB of HBM per device.

v0:
```python
import jax
import jax.numpy as jnp
from jax import lax
from jax.sharding import PartitionSpec as P

TILE = 128


TAU = 0.12
NEG = -1e30
EPS = 1e-06


def masked_scores(rows_q, rows_k, mask_rows, first):
    s = jnp.einsum("qd,kd->qk", rows_q, rows_k, preferred_element_type=jnp.float32) / TAU
    nq, nk = s.shape
    ids = first + jnp.arange(nk // TILE, dtype=jnp.int32)
    hit = jnp.any(mask_rows[:, :, None] == ids[None, None, :], axis=1)
    live = jnp.broadcast_to(
        jnp.logical_not(hit)[:, None, :, None], (nq // TILE, TILE, nk // TILE, TILE)
    ).reshape(nq, nk)
    return (jnp.where(live, s, NEG), live)


def on_device(bank, queries, keys, labels, mask_tiles):
    qdev = queries.shape[0]
    bdev = bank.shape[0]
    total_bank = bdev * lax.axis_size("bank")
    total_query = qdev * lax.axis_size("batch")
    eta = 0.25 * total_bank / total_query
    mine = lax.axis_index("batch")
    first = lax.axis_index("bank") * (bdev // TILE)
    all_keys = lax.all_gather(keys, "batch", axis=0, tiled=True)
    key_rows = jnp.take(all_keys, labels, axis=0)
    pos = jnp.sum(queries.astype(jnp.float32) * key_rows.astype(jnp.float32), axis=1) / TAU
    own_mask = lax.dynamic_slice_in_dim(mask_tiles, mine * (qdev // TILE), qdev // TILE, 0)
    scores, live = masked_scores(queries, bank, own_mask, first)
    top = lax.pmax(jnp.max(scores, axis=1), "bank")
    part_sum = jnp.sum(jnp.where(live, jnp.exp(scores - top[:, None]), 0.0), axis=1)
    total = lax.psum(part_sum, "bank")
    high = jnp.maximum(top, pos)
    lse = high + jnp.log(total * jnp.exp(top - high) + jnp.exp(pos - high))
    loss = lse - pos
    probs = jnp.exp(scores - lse[:, None]).astype(jnp.bfloat16)
    neg_local = jnp.dot(probs, bank, preferred_element_type=jnp.float32)
    own_pull = jnp.einsum("qk,qd->kd", probs, queries, preferred_element_type=jnp.float32)
    neg = lax.psum(neg_local, "bank")
    query_grad = (neg + (jnp.exp(pos - lse) - 1.0)[:, None] * key_rows.astype(jnp.float32)) / TAU
    pull = lax.psum(own_pull.astype(jnp.bfloat16), "batch").astype(jnp.float32)
    fresh = bank.astype(jnp.float32) + eta * pull
    fresh = fresh * lax.rsqrt(jnp.mean(fresh * fresh, axis=1, keepdims=True) + EPS)
    return (fresh.astype(jnp.bfloat16), query_grad, loss)


def solution(mesh):
    return jax.shard_map(
        on_device,
        mesh=mesh,
        in_specs=(
            P(("parts", "bank"), None),
            P(("parts", "batch"), None),
            P(("parts", "batch"), None),
            P(("parts", "batch")),
            P("parts", None),
        ),
        out_specs=(P(("parts", "bank"), None), P(("parts", "batch"), None), P(("parts", "batch"))),
        check_vma=False,
    )
```

profile of v0, /device:TPU:0, one launch (start us, length us, event | category | flops | bytes accessed | tf_op | source)
XLA Modules:
  0.0 187.6 jit_solution(10827751201215872760)
XLA Ops:
  7.2 0.0 copy-start
  7.2 0.0 all-gather.2.cloned.1.call-start
  7.2 0.7 all-gather.2.cloned.1.call-update
  7.9 0.0 all-reduce.3.cloned.1.call-start
  8.0 0.0 copy-done
  8.0 0.1 compare_reduce_fusion
  8.1 0.6 broadcast_in_dim.31
  8.7 6.8 %fusion = (f32[1024]{0:T(1024)S(1)}, f32[1024,2048]{1,0:T(8,128)}) fusion(pred[128,8,16,128]{3,2,1,0:T(8,128)(4,1)S(1)} %bitcast.17, bf16[1024,256]{1,0:T(8,128)(2,1)} %param.6, bf16[2048,256]{1,0:T(8,128)(2,1)} %param.5), kind=kOutput, calls=%fused_computation.4 | convolution fusion | flops 1080032256 | bytes 12062720 | tf_op jit(solution)/shard_map/qd,kd->qk/dot_general | solution.py:15
  15.5 23.1 %pmax.7 = f32[1024]{0:T(1024)S(1)} all-reduce(f32[1024]{0:T(1024)S(1)} %get-tuple-element.5), channel_id=1, replica_groups=mesh['parts'=2,'bank'=8,'batch'=2] {'bank'}, use_global_device_ids=true, to_apply=%region_2.3 | all-reduce | flops 1024 | bytes 8192 | tf_op jit(solution)/shard_map/pmax | solution.py:38
  38.6 0.0 copy-start.4
  38.6 5.3 %select_reduce_fusion = f32[1024]{0:T(1024)S(1)} fusion(pred[128,8,16,128]{3,2,1,0:T(8,128)(4,1)S(1)} %bitcast.18, f32[1024,2048]{1,0:T(8,128)} %get-tuple-element.6, f32[1024]{0:T(1024)S(1)} %pmax.7), kind=kLoop, calls=%fused_computation.2 | loop fusion | flops 10484736 | bytes 10493952 | tf_op jit(solution)/shard_map/reduce_sum | solution.py:39
  43.9 0.0 copy-start.3
  43.9 17.3 %psum.21 = f32[1024]{0:T(1024)S(1)} all-reduce(f32[1024]{0:T(1024)S(1)} %select_reduce_fusion), channel_id=1, replica_groups=mesh['parts'=2,'bank'=8,'batch'=2] {'bank'}, use_global_device_ids=true, to_apply=%region_5.6 | all-reduce | flops 1024 | bytes 8192 | tf_op jit(solution)/shard_map/psum | solution.py:40
  61.2 0.0 copy-done.4
  61.2 0.0 all-gather.2.cloned.1.call-done
  61.2 4.8 %gather_fusion = bf16[1024,256]{1,0:T(8,128)(2,1)S(1)} fusion(bf16[2048,256]{1,0:T(8,128)(2,1)} %all-gather.2.cloned.1.call-done, s32[1024]{0:T(1024)S(1)} %fusion.6), kind=kCustom, calls=%fused_computation | custom fusion | bytes 1052672 | tf_op jit(solution)/shard_map/jit(_take)/gather | solution.py:34
  66.1 0.0 copy-done.3
  66.1 0.5 fusion.1
  66.6 0.6 multiply_subtract_fusion
  67.2 5.5 %exponential_convert_fusion = bf16[1024,2048]{1,0:T(8,128)(2,1)S(1)} fusion(f32[1024,2048]{1,0:T(8,128)} %get-tuple-element.6, pred[128,8,16,128]{3,2,1,0:T(8,128)(4,1)S(1)} %bitcast.19, f32[1024]{0:T(1024)S(1)} %get-tuple-element.4), kind=kLoop, calls=%fused_computation.1 | loop fusion | flops 8388608 | bytes 14684160 | tf_op jit(solution)/shard_map/convert_element_type | solution.py:44
  72.7 0.0 copy-start.2
  72.7 1.9 %copy-done.2 = bf16[1024,2048]{1,0:T(8,128)(2,1)} copy-done((bf16[1024,2048]{1,0:T(8,128)(2,1)}, bf16[1024,2048]{1,0:T(8,128)(2,1)S(1)}, u32[]{:S(2)}) %copy-start.2) | copy-done | bytes 4194328
  74.6 0.0 copy-start.1
  74.6 2.4 %convolution_convert_fusion = bf16[2048,256]{1,0:T(8,128)(2,1)} fusion(bf16[1024,2048]{1,0:T(8,128)(2,1)S(1)} %exponential_convert_fusion, bf16[1024,256]{1,0:T(8,128)(2,1)S(1)} %copy-done.3), kind=kOutput, calls=%fused_computation.5 | convolution fusion | flops 1074266112 | bytes 5767168 | tf_op jit(solution)/shard_map/qk,qd->kd/dot_general | solution.py:46
  77.0 0.0 all-reduce.3.cloned.1.call-update
  77.0 0.0 all-reduce.5.cloned.1.call-start
  77.0 0.0 copy-done.1
  77.0 4.5 %fusion.7 = f32[1024,256]{1,0:T(8,128)} fusion(bf16[1024,2048]{1,0:T(8,128)(2,1)} %copy-done.2, bf16[2048,256]{1,0:T(8,128)(2,1)S(1)} %copy-done.1), kind=kOutput, calls=%fused_computation.28 | convolution fusion | flops 1073741824 | bytes 6291456 | tf_op jit(solution)/shard_map/dot_general | solution.py:45
  81.5 0.0 all-reduce.5.cloned.1.call-update
  81.6 13.9 %all-reduce.3.cloned.1.call-done = bf16[2048,256]{1,0:T(8,128)(2,1)} async-done(((bf16[2048,256]{1,0:T(8,128)(2,1)}), bf16[2048,256]{1,0:T(8,128)(2,1)}) %all-reduce.3.cloned.1.call-update) | async-done | bytes 1048592 | tf_op jit(solution)/shard_map/psum | solution.py:49
  95.5 1.7 multiply_reduce_fusion
  97.2 2.6 %multiply_convert_fusion = bf16[2048,256]{1,0:T(8,128)(2,1)} fusion(bf16[2048,256]{1,0:T(8,128)(2,1)} %all-reduce.3.cloned.1.call-done, bf16[2048,256]{1,0:T(8,128)(2,1)S(1)} %copy-done.1, f32[2048]{0:T(1024)S(1)} %add_rsqrt_fusion), kind=kLoop, calls=%fused_computation.6 | loop fusion | flops 3145728 | bytes 3153920 | tf_op jit(solution)/shard_map/convert_element_type | solution.py:52
  99.8 78.7 %all-reduce.5.cloned.1.call-done = f32[1024,256]{1,0:T(8,128)} async-done(((f32[1024,256]{1,0:T(8,128)}), f32[1024,256]{1,0:T(8,128)}) %all-reduce.5.cloned.1.call-update) | async-done | bytes 1048592 | tf_op jit(solution)/shard_map/psum | solution.py:47
  178.6 2.5 %fusion.3 = f32[1024,256]{1,0:T(8,128)} fusion(f32[1024,256]{1,0:T(8,128)} %all-reduce.5.cloned.1.call-done, f32[1024]{0:T(1024)S(1)} %exponential_add_fusion, bf16[1024,256]{1,0:T(8,128)(2,1)S(1)} %gather_fusion, pred[1024]{0:T(1024)(128)(4,1)S(1)} %compare_and_fusion), kind=kLoop, calls=%fused_computation.13 | loop fusion | flops 1310720 | bytes 2626560 | tf_op jit(solution)/shard_map/div | solution.py:48
  (7 shorter events, 0.1 us)
Async XLA Ops:
  7.2 0.8 copy-start
  7.2 54.1 %all-gather.2.cloned.1.call-start = ((), (), s32[]{:S(2)}) async-start(), calls=%async_computation | async-start | bytes 1572864 | tf_op jit(solution)/shard_map/all_gather | solution.py:33
  7.9 87.6 %all-reduce.3.cloned.1.call-start = ((), (), s32[]{:S(2)}) async-start(), calls=%async_computation.1 | async-start | bytes 2097152 | tf_op jit(solution)/shard_map/psum | solution.py:49
  38.6 22.6 %copy-start.4 = (s32[1024]{0:T(1024)S(1)}, s32[1024]{0:T(1024)}, u32[]{:S(2)}) copy-start(s32[1024]{0:T(1024)} %param.8) | copy-start | bytes 12292
  43.9 22.2 %copy-start.3 = (bf16[1024,256]{1,0:T(8,128)(2,1)S(1)}, bf16[1024,256]{1,0:T(8,128)(2,1)}, u32[]{:S(2)}) copy-start(bf16[1024,256]{1,0:T(8,128)(2,1)} %param.6) | copy-start | bytes 1572868
  72.7 1.9 %copy-start.2 = (bf16[1024,2048]{1,0:T(8,128)(2,1)}, bf16[1024,2048]{1,0:T(8,128)(2,1)S(1)}, u32[]{:S(2)}) copy-start(bf16[1024,2048]{1,0:T(8,128)(2,1)S(1)} %exponential_convert_fusion) | copy-start | bytes 12582916
  74.6 2.4 %copy-start.1 = (bf16[2048,256]{1,0:T(8,128)(2,1)S(1)}, bf16[2048,256]{1,0:T(8,128)(2,1)}, u32[]{:S(2)}) copy-start(bf16[2048,256]{1,0:T(8,128)(2,1)} %param.5) | copy-start | bytes 3145732
  77.0 101.6 %all-reduce.5.cloned.1.call-start = ((), (), s32[]{:S(2)}) async-start(), calls=%async_computation.2 | async-start | bytes 2097152 | tf_op jit(solution)/shard_map/psum | solution.py:47
Sparse Core Ops, SparseCore 0:
  9.6 11.7 all-gather.1
  77.1 18.3 all-reduce.2
  99.4 79.1 all-reduce.4
where the time goes:
time: 188 us
  waiting for transfers between devices  93.4 us (50%)
  blocking collectives  40.3 us (21%)
  other arithmetic  18.9 us (10%)
  between operations  13.9 us (7%)
  matrix products  13.6 us (7%)
  local copies, waits for them, and re-layouts  7.38 us (4%)
    psum x1, waiting for transfers between devices, on_device(): neg = lax.psum(neg_local, 'bank')  78.7 us
    pmax x1, blocking collectives, on_device(): top = lax.pmax(jnp.max(scores, axis=1), 'bank')  23.1 us
    psum x1, blocking collectives, on_device(): total = lax.psum(part_sum, 'bank')  17.3 us
    psum x1, waiting for transfers between devices, on_device(): pull = lax.psum(own_pull.astype(jnp.bfloat16), 'batch').astype(jnp.float32)  13.9 us
    dot_general x1, matrix products, masked_scores(): jnp.einsum('qd,kd->qk', rows_q, rows_k, preferred_element_type=jnp.float32)  6.76 us
    convert_element_type x1, other arithmetic, on_device(): probs = jnp.exp(scores - lse[:, None]).astype(jnp.bfloat16)  5.45 us
    reduce_sum x1, other arithmetic, on_device(): jnp.sum(jnp.where(live, jnp.exp(scores - top[:, None]), 0.0), axis=1)  5.32 us
    gather x1, local copies, waits for them, and re-layouts, on_device(): key_rows = jnp.take(all_keys, labels, axis=0)  4.82 us
  transfers between devices with their start and end apart: 3, of which 2 were waited for; matrix products, arithmetic and copies ran while one was open for 12% of the time, Pallas kernels for 0%

commit v1 on v0

--- a/solution.py
+++ b/solution.py
@@ -1,6 +1,11 @@
+import functools
+import math
+
 import jax
 import jax.numpy as jnp
 from jax import lax
+from jax.experimental import pallas as pl
+from jax.experimental.pallas import tpu as pltpu
 from jax.sharding import PartitionSpec as P
 
 TILE = 128
@@ -8,7 +13,14 @@
 
 TAU = 0.12
 NEG = -1e30
+FLOOR = -1e29
 EPS = 1e-06
+LOG2E = math.log2(math.e)
+LN2 = math.log(2.0)
+SCALE2 = LOG2E / TAU
+QCH = 256
+BCH = 256
+MESH = pl.DeviceIdType.MESH
 
 
 def masked_scores(rows_q, rows_k, mask_rows, first):
@@ -22,7 +34,7 @@
     return (jnp.where(live, s, NEG), live)
 
 
-def on_device(bank, queries, keys, labels, mask_tiles):
+def general(bank, queries, keys, labels, mask_tiles):
     qdev = queries.shape[0]
     bdev = bank.shape[0]
     total_bank = bdev * lax.axis_size("bank")
@@ -52,6 +64,220 @@
     return (fresh.astype(jnp.bfloat16), query_grad, loss)
 
 
+def column(row):
+    return jnp.transpose(jnp.broadcast_to(row, (TILE, TILE)))
+
+
+def wide_column(row, width):
+    return jnp.concatenate([column(row)] * (width // TILE), axis=1)
+
+
+def step_kernel(
+    n, eta, mask_ref, bank_ref, q_ref, keys_ref, labels_ref,
+    new_ref, grad_ref, loss_ref,
+    s_scr, p_scr, bankt_scr, bias_scr, neg_scr, keys_scr, stats_scr, qs_scr,
+    stage_scr, rs_scr, pull_scr, pull_in_scr,
+    keys_sems, stats_send, stats_recv, rs_send, rs_recv, ag_send, ag_recv, pull_send, pull_recv,
+):
+    me = lax.axis_index("bank")
+    mine = lax.axis_index("batch")
+    other = 1 - mine
+    bdev, width = bank_ref.shape
+    qdev = q_ref.shape[0]
+    tiles = bdev // TILE
+    blocks = qdev // TILE
+    listed = mask_ref.shape[1]
+    first = me * tiles
+
+    barrier = pltpu.get_barrier_semaphore()
+    for d in range(1, n):
+        pl.semaphore_signal(barrier, inc=1, device_id={"bank": lax.rem(me + d, n)}, device_id_type=MESH)
+    pl.semaphore_signal(barrier, inc=1, device_id={"batch": other}, device_id_type=MESH)
+
+    ids = first + lax.broadcasted_iota(jnp.int32, (tiles, TILE), 0)
+    for b in range(blocks):
+        hit = ids == mask_ref[mine * blocks + b, 0]
+        for m in range(1, listed):
+            hit = jnp.logical_or(hit, ids == mask_ref[mine * blocks + b, m])
+        bias_scr[:, b * TILE:(b + 1) * TILE] = jnp.where(hit, NEG, 0.0)
+
+    for k in range(bdev // BCH):
+        bankt_scr[:, k * BCH:(k + 1) * BCH] = jnp.transpose(bank_ref[k * BCH:(k + 1) * BCH, :])
+
+    def keys_copy():
+        return pltpu.make_async_remote_copy(
+            src_ref=keys_ref, dst_ref=keys_scr, send_sem=keys_sems.at[0], recv_sem=keys_sems.at[1],
+            device_id={"batch": other}, device_id_type=MESH)
+
+    for c in range(qdev // QCH):
+        cols = slice(c * QCH, (c + 1) * QCH)
+        qc = q_ref[cols, :]
+        top8 = jnp.full((8, QCH), FLOOR, jnp.float32)
+        for k in range(bdev // BCH):
+            s = lax.dot_general(bank_ref[k * BCH:(k + 1) * BCH, :], qc, (((1,), (1,)), ((), ())),
+                                preferred_element_type=jnp.float32)
+            for t in range(BCH // TILE):
+                tile = k * (BCH // TILE) + t
+                part = s[t * TILE:(t + 1) * TILE, :] * SCALE2 + bias_scr[tile:tile + 1, cols]
+                s_scr[c % 2, tile * TILE:(tile + 1) * TILE, :] = part
+                top8 = jnp.maximum(top8, jnp.max(part.reshape(TILE // 8, 8, QCH), axis=0))
+        top = jnp.max(top8, axis=0, keepdims=True)
+        sum8 = jnp.zeros((8, QCH), jnp.float32)
+        for tile in range(tiles):
+            rows = slice(tile * TILE, (tile + 1) * TILE)
+            p = jnp.exp2(s_scr[c % 2, rows, :] - top)
+            sum8 = sum8 + jnp.sum(p.reshape(TILE // 8, 8, QCH), axis=0)
+            p_scr[rows, cols] = p.astype(jnp.bfloat16)
+        total = jnp.sum(sum8, axis=0, keepdims=True)
+        for t in range(QCH // TILE):
+            b = c * (QCH // TILE) + t
+            stats_scr[me, b:b + 1, :] = top[:, t * TILE:(t + 1) * TILE]
+            stats_scr[me, 8 + b:9 + b, :] = total[:, t * TILE:(t + 1) * TILE]
+        if c == 0:
+            pl.semaphore_wait(barrier, n)
+            keys_copy().start()
+
+    own = pl.ds(pl.multiple_of(me * TILE, TILE), TILE)
+    label_row = labels_ref[pl.ds(me, 1), :]
+    row_ids = lax.broadcasted_iota(jnp.int32, (qdev, TILE), 0)
+
+    def picked(table, start):
+        hot = jnp.where(row_ids + start == label_row, 1.0, 0.0).astype(jnp.bfloat16)
+        return lax.dot_general(hot, table, (((0,), (0,)), ((), ())), preferred_element_type=jnp.float32)
+
+    key_rows = picked(keys_ref[...], mine * qdev)
+    keys_copy().wait()
+    key_rows = key_rows + picked(keys_scr[...], other * qdev)
+    prod = q_ref[own, :].astype(jnp.float32) * key_rows
+    own_pos = jnp.sum(jnp.transpose(prod), axis=0, keepdims=True) / TAU
+    stats_scr[me, 16:24, :] = jnp.broadcast_to(own_pos, (8, TILE))
+
+    def to_peer(d, src, dst, send, recv):
+        return pltpu.make_async_remote_copy(
+            src_ref=src, dst_ref=dst, send_sem=send.at[d], recv_sem=recv.at[d],
+            device_id={"bank": lax.rem(me + d, n)}, device_id_type=MESH)
+
+    stats = [to_peer(d, stats_scr.at[me], stats_scr.at[me], stats_send, stats_recv) for d in range(1, n)]
+    for copy in stats:
+        copy.start()
+
+    for c in range(qdev // QCH):
+        cols = slice(c * QCH, (c + 1) * QCH)
+        neg_scr[:, cols] = jnp.dot(bankt_scr[...], p_scr[:, cols], preferred_element_type=jnp.float32)
+
+    for copy in stats:
+        copy.wait()
+    high = jnp.concatenate([stats_scr[b, 16:17, :] for b in range(n)], axis=0) * LOG2E
+    pos = high
+    for b in range(n):
+        high = jnp.maximum(high, stats_scr[b, 0:8, :])
+    total = jnp.exp2(pos - high)
+    for b in range(n):
+        total = total + stats_scr[b, 8:16, :] * jnp.exp2(stats_scr[b, 0:8, :] - high)
+    lse = high + jnp.log(total) * LOG2E
+    loss_ref[...] = (lse - pos) * LN2
+    alpha = jnp.exp2(stats_scr[me, 0:8, :] - lse)
+
+    for b in range(blocks):
+        stage_scr[b] = (neg_scr[:, b * TILE:(b + 1) * TILE] * alpha[b:b + 1, :]).astype(jnp.bfloat16)
+    scatter = []
+    for d in range(1, n):
+        copy = to_peer(d, stage_scr.at[lax.rem(me + d, n)], rs_scr.at[d], rs_send, rs_recv)
+        copy.start()
+        scatter.append(copy)
+
+    for b in range(blocks):
+        rows = slice(b * TILE, (b + 1) * TILE)
+        qs_scr[rows, :] = (q_ref[rows, :].astype(jnp.float32) * wide_column(alpha[b:b + 1, :], width)).astype(jnp.bfloat16)
+    exchange = []
+    for k in range(bdev // BCH):
+        rows = slice(k * BCH, (k + 1) * BCH)
+        pull_scr[rows, :] = jnp.dot(p_scr[rows, :], qs_scr[...], preferred_element_type=jnp.float32).astype(jnp.bfloat16)
+        copy = pltpu.make_async_remote_copy(
+            src_ref=pull_scr.at[rows, :], dst_ref=pull_in_scr.at[rows, :],
+            send_sem=pull_send.at[k], recv_sem=pull_recv.at[k],
+            device_id={"batch": other}, device_id_type=MESH)
+        copy.start()
+        exchange.append(copy)
+
+    row_of = lax.broadcasted_iota(jnp.int32, (n, TILE), 0) == me
+    factor = jnp.sum(jnp.where(row_of, jnp.exp2(pos - lse) - 1.0, 0.0), axis=0, keepdims=True)
+    negs = stage_scr[me].astype(jnp.float32)
+    for d in range(1, n):
+        scatter[d - 1].wait()
+        negs = negs + rs_scr[d].astype(jnp.float32)
+    grad = (jnp.transpose(negs) + wide_column(factor, width) * key_rows) / TAU
+    grad_ref[me] = grad.astype(jnp.bfloat16)
+    gather = []
+    for d in range(1, n):
+        copy = to_peer(d, grad_ref.at[me], grad_ref.at[me], ag_send, ag_recv)
+        copy.start()
+        gather.append(copy)
+
+    for k in range(bdev // BCH):
+        rows = slice(k * BCH, (k + 1) * BCH)
+        exchange[k].wait()
+        pull = pull_scr[rows, :].astype(jnp.float32) + pull_in_scr[rows, :].astype(jnp.float32)
+        fresh = bank_ref[rows, :].astype(jnp.float32) + eta * pull
+        fresh = fresh * lax.rsqrt(jnp.mean(fresh * fresh, axis=1, keepdims=True) + EPS)
+        new_ref[rows, :] = fresh.astype(jnp.bfloat16)
+    for copy in gather:
+        copy.wait()
+
+
+def fused(bank, queries, keys, labels, mask_tiles):
+    n = lax.axis_size("bank")
+    qdev, width = queries.shape
+    bdev = bank.shape[0]
+    eta = 0.25 * (bdev * n) / (qdev * lax.axis_size("batch"))
+    vmem = pl.BlockSpec(memory_space=pltpu.VMEM)
+    dma = pltpu.SemaphoreType.DMA
+    new_bank, grad, loss = pl.pallas_call(
+        functools.partial(step_kernel, n, eta),
+        out_shape=(
+            jax.ShapeDtypeStruct((bdev, width), jnp.bfloat16),
+            jax.ShapeDtypeStruct((n, TILE, width), jnp.bfloat16),
+            jax.ShapeDtypeStruct((n, TILE), jnp.float32),
+        ),
+        in_specs=[pl.BlockSpec(memory_space=pltpu.SMEM)] + [vmem] * 4,
+        out_specs=(vmem, vmem, vmem),
+        scratch_shapes=[
+            pltpu.VMEM((2, bdev, QCH), jnp.float32),
+            pltpu.VMEM((bdev, qdev), jnp.bfloat16),
+            pltpu.VMEM((width, bdev), jnp.bfloat16),
+            pltpu.VMEM((bdev // TILE, qdev), jnp.float32),
+            pltpu.VMEM((width, qdev), jnp.float32),
+            pltpu.VMEM((qdev, width), jnp.bfloat16),
+            pltpu.VMEM((n, 24, TILE), jnp.float32),
+            pltpu.VMEM((qdev, width), jnp.bfloat16),
+            pltpu.VMEM((n, width, TILE), jnp.bfloat16),
+            pltpu.VMEM((n, width, TILE), jnp.bfloat16),
+            pltpu.VMEM((bdev, width), jnp.bfloat16),
+            pltpu.VMEM((bdev, width), jnp.bfloat16),
+            dma((2,)),
+            dma((n,)), dma((n,)),
+            dma((n,)), dma((n,)),
+            dma((n,)), dma((n,)),
+            dma((bdev // BCH,)), dma((bdev // BCH,)),
+        ],
+        compiler_params=pltpu.CompilerParams(
+            collective_id=0, has_side_effects=True, vmem_limit_bytes=48 * 1024 * 1024
+        ),
+    )(mask_tiles, bank, queries, keys, labels.reshape(n, TILE))
+    return (new_bank, grad.reshape(qdev, width).astype(jnp.float32), loss.reshape(qdev))
+
+
+def on_device(bank, queries, keys, labels, mask_tiles):
+    n = lax.axis_size("bank")
+    fits = (
+        n == 8
+        and queries.shape[0] == n * TILE
+        and bank.shape[0] % BCH == 0
+        and lax.axis_size("batch") == 2
+    )
+    return (fused if fits else general)(bank, queries, keys, labels, mask_tiles)
+
+
 def solution(mesh):
     return jax.shard_map(
         on_device,

time: 188 us -> 44.9 us (0.24)
  waiting for transfers between devices: 93.4 us -> 0 us
  blocking collectives: 40.3 us -> 0 us
  Pallas kernels: 0 us -> 36.6 us
  other arithmetic: 18.9 us -> 1.08 us
  matrix products: 13.6 us -> 0 us
  between operations: 13.9 us -> 0.65 us
    psum x2 -> x0, waiting for transfers between devices: 92.6 us -> none  [the longest x1 78.7 us: on_device(): neg = lax.psum(neg_local, 'bank')]
    pallas_call x0 -> x1, Pallas kernels: none -> 36.6 us  [fused(): pl.pallas_call(functools.partial(step_kernel, n, eta), out_shape=(jax.Sha...]
    pmax x1 -> x0, blocking collectives: 23.1 us -> none  [on_device(): top = lax.pmax(jnp.max(scores, axis=1), 'bank')]
    psum x1 -> x0, blocking collectives: 17.3 us -> none  [on_device(): total = lax.psum(part_sum, 'bank')]
    dot_general x3 -> x0, matrix products: 13.6 us -> none  [the longest x1 6.76 us: masked_scores(): jnp.einsum('qd,kd->qk', rows_q, rows_k, preferred_element_type=jnp.float32)]
    reduce_sum x3 -> x0, other arithmetic: 7.56 us -> none  [the longest x1 5.32 us: on_device(): jnp.sum(jnp.where(live, jnp.exp(scores - top[:, None]), 0.0), axis=1)]
    convert_element_type x2 -> x1, other arithmetic: 8.08 us -> 1.08 us  [fused(): grad.reshape(qdev, width).astype(jnp.float32)]
    gather x1 -> x0, local copies, waits for them, and re-layouts: 4.82 us -> none  [on_device(): key_rows = jnp.take(all_keys, labels, axis=0)]
  transfers between devices with their start and end apart: 3 -> 0, of which waited for: 2 -> 0; matrix products, arithmetic and copies ran while one was open for 12% -> 0% of each run, Pallas kernels for 0% -> 0%
where the time goes in v1:
time: 44.9 us; the launch traced here: 44.6 us
  Pallas kernels  36.6 us (82%)
  local copies, waits for them, and re-layouts  6.25 us (14%)
  other arithmetic  1.08 us (2%)
  between operations  0.65 us (1%)
    pallas_call x1, Pallas kernels, fused(): pl.pallas_call(functools.partial(step_kernel, n, eta), out_shape=(jax.Sha...  36.6 us
    unnamed x12, local copies, waits for them, and re-layouts  6.25 us
    convert_element_type x1, other arithmetic, fused(): grad.reshape(qdev, width).astype(jnp.float32)  1.08 us

profile of v1, /device:TPU:0, one launch (start us, length us, event | category | flops | bytes accessed | tf_op | source)
XLA Modules:
  0.0 44.6 jit_solution(15988206593561055025)
XLA Ops:
  0.6 0.0 copy-start
  0.6 1.2 %copy-done = bf16[2048,256]{1,0:T(8,128)(2,1)S(1)} copy-done((bf16[2048,256]{1,0:T(8,128)(2,1)S(1)}, bf16[2048,256]{1,0:T(8,128)(2,1)}, u32[]{:S(2)}) %copy-start) | copy-done | bytes 1048600
  1.9 0.0 copy-start.1
  1.9 1.0 %copy-done.1 = bf16[1024,256]{1,0:T(8,128)(2,1)S(1)} copy-done((bf16[1024,256]{1,0:T(8,128)(2,1)S(1)}, bf16[1024,256]{1,0:T(8,128)(2,1)}, u32[]{:S(2)}) %copy-start.1) | copy-done | bytes 524312
  2.9 0.0 copy-start.2
  2.9 1.0 %copy-done.2 = bf16[1024,256]{1,0:T(8,128)(2,1)S(1)} copy-done((bf16[1024,256]{1,0:T(8,128)(2,1)S(1)}, bf16[1024,256]{1,0:T(8,128)(2,1)}, u32[]{:S(2)}) %copy-start.2) | copy-done | bytes 524312
  3.9 0.0 copy-start.3
  3.9 0.7 %copy-done.3 = s32[16,16]{1,0:T(8,128)S(1)} copy-done((s32[16,16]{1,0:T(8,128)S(1)}, s32[16,16]{1,0:T(8,128)}, u32[]{:S(2)}) %copy-start.3) | copy-done | bytes 1048
  4.6 0.0 copy-start.4
  4.6 0.7 %copy-done.4 = s32[1024]{0:T(1024)S(1)} copy-done((s32[1024]{0:T(1024)S(1)}, s32[1024]{0:T(1024)}, u32[]{:S(2)}) %copy-start.4) | copy-done | bytes 4120
  5.3 36.6 %shard_map.76 = (bf16[2048,256]{1,0:T(8,128)(2,1)S(1)}, bf16[8,128,256]{2,1,0:T(8,128)(2,1)S(1)}, f32[8,128]{1,0:T(8,128)S(1)}) custom-call(s32[16,16]{1,0:T(8,128)S(1)} %copy-done.3, bf16[2048,256]{1,0:T(8,128)(2,1)S(1)} %copy-done, bf16[1024,256]{1,0:T(8,128)(2,1)S(1)} %copy-done.1, bf16[1024,256]{1,0:T(8,128)(2,1)S(1)} %copy-done.2, s32[8,128]{1,0:T(8,128)S(1)} %bitcast.5), custom_call_target="tpu_custom_call" | custom-call | tf_op jit(solution)/shard_map/pallas_call | solution.py:235
  41.9 1.1 %bitcast_convert_fusion = f32[1024,256]{1,0:T(8,128)} fusion(bf16[8,128,256]{2,1,0:T(8,128)(2,1)S(1)} %get-tuple-element.7), kind=kLoop, calls=%fused_computation | loop fusion | flops 262144 | bytes 1572864 | tf_op jit(solution)/shard_map/convert_element_type | solution.py:267
  43.0 1.0 %copy.10 = bf16[2048,256]{1,0:T(8,128)(2,1)} copy(bf16[2048,256]{1,0:T(8,128)(2,1)S(1)} %get-tuple-element.12) | data formatting | bytes 2097152
  44.0 0.6 %copy.11 = f32[1024]{0:T(1024)} copy(f32[1024]{0:T(1024)S(1)} %bitcast.6) | data formatting | bytes 8192
Async XLA Ops:
  0.6 1.2 %copy-start = (bf16[2048,256]{1,0:T(8,128)(2,1)S(1)}, bf16[2048,256]{1,0:T(8,128)(2,1)}, u32[]{:S(2)}) copy-start(bf16[2048,256]{1,0:T(8,128)(2,1)} %bank_ref.1) | copy-start | bytes 3145732
  1.9 1.0 %copy-start.1 = (bf16[1024,256]{1,0:T(8,128)(2,1)S(1)}, bf16[1024,256]{1,0:T(8,128)(2,1)}, u32[]{:S(2)}) copy-start(bf16[1024,256]{1,0:T(8,128)(2,1)} %q_ref.1) | copy-start | bytes 1572868
  2.9 1.0 %copy-start.2 = (bf16[1024,256]{1,0:T(8,128)(2,1)S(1)}, bf16[1024,256]{1,0:T(8,128)(2,1)}, u32[]{:S(2)}) copy-start(bf16[1024,256]{1,0:T(8,128)(2,1)} %keys_ref.1) | copy-start | bytes 1572868
  3.9 0.7 %copy-start.3 = (s32[16,16]{1,0:T(8,128)S(1)}, s32[16,16]{1,0:T(8,128)}, u32[]{:S(2)}) copy-start(s32[16,16]{1,0:T(8,128)} %mask_ref.1) | copy-start | bytes 3076
  4.6 0.7 %copy-start.4 = (s32[1024]{0:T(1024)S(1)}, s32[1024]{0:T(1024)}, u32[]{:S(2)}) copy-start(s32[1024]{0:T(1024)} %param.8) | copy-start | bytes 12292

commit v2 on v1

--- a/solution.py
+++ b/solution.py
@@ -73,11 +73,12 @@
 
 
 def step_kernel(
-    n, eta, mask_ref, bank_ref, q_ref, keys_ref, labels_ref,
+    n, eta, mask_hbm, bank_hbm, q_hbm, keys_hbm, labels_hbm,
     new_ref, grad_ref, loss_ref,
-    s_scr, p_scr, bankt_scr, bias_scr, neg_scr, keys_scr, stats_scr, qs_scr,
+    mask_ref, bank_ref, q_ref, keys_ref, labels_ref,
+    s_scr, p_scr, bankt_scr, bias_scr, keys_scr, stats_scr, qs_scr,
     stage_scr, rs_scr, pull_scr, pull_in_scr,
-    keys_sems, stats_send, stats_recv, rs_send, rs_recv, ag_send, ag_recv, pull_send, pull_recv,
+    in_sems, keys_sems, stats_send, stats_recv, rs_send, rs_recv, ag_send, ag_recv, pull_send, pull_recv,
 ):
     me = lax.axis_index("bank")
     mine = lax.axis_index("batch")
@@ -88,29 +89,51 @@
     blocks = qdev // TILE
     listed = mask_ref.shape[1]
     first = me * tiles
+    levels = n // 2
+    z = me // 2
+    x = lax.rem(me, 2)
+
+    loads = [
+        pltpu.make_async_copy(src, dst, in_sems.at[i])
+        for i, (src, dst) in enumerate((
+            (mask_hbm, mask_ref), (bank_hbm, bank_ref), (q_hbm, q_ref), (labels_hbm, labels_ref), (keys_hbm, keys_ref)))
+    ]
+    for load in loads:
+        load.start()
 
     barrier = pltpu.get_barrier_semaphore()
     for d in range(1, n):
         pl.semaphore_signal(barrier, inc=1, device_id={"bank": lax.rem(me + d, n)}, device_id_type=MESH)
     pl.semaphore_signal(barrier, inc=1, device_id={"batch": other}, device_id_type=MESH)
 
+    loads[0].wait()
     ids = first + lax.broadcasted_iota(jnp.int32, (tiles, TILE), 0)
     for b in range(blocks):
         hit = ids == mask_ref[mine * blocks + b, 0]
         for m in range(1, listed):
             hit = jnp.logical_or(hit, ids == mask_ref[mine * blocks + b, m])
-        bias_scr[:, b * TILE:(b + 1) * TILE] = jnp.where(hit, NEG, 0.0)
-
+        bias_scr[b] = jnp.where(hit, NEG, 0.0)
+
+    loads[1].wait()
     for k in range(bdev // BCH):
         bankt_scr[:, k * BCH:(k + 1) * BCH] = jnp.transpose(bank_ref[k * BCH:(k + 1) * BCH, :])
+    loads[2].wait()
 
     def keys_copy():
         return pltpu.make_async_remote_copy(
-            src_ref=keys_ref, dst_ref=keys_scr, send_sem=keys_sems.at[0], recv_sem=keys_sems.at[1],
+            src_ref=keys_hbm, dst_ref=keys_scr, send_sem=keys_sems.at[0], recv_sem=keys_sems.at[1],
             device_id={"batch": other}, device_id_type=MESH)
 
-    for c in range(qdev // QCH):
-        cols = slice(c * QCH, (c + 1) * QCH)
+    def to_bank(peer, src, dst, send, recv):
+        return pltpu.make_async_remote_copy(
+            src_ref=src, dst_ref=dst, send_sem=send, recv_sem=recv,
+            device_id={"bank": peer}, device_id_type=MESH)
+
+    half = QCH // TILE
+    scatter = []
+    for step in range(levels):
+        c = lax.rem(z + step + 1, levels)
+        cols = pl.ds(pl.multiple_of(c * QCH, QCH), QCH)
         qc = q_ref[cols, :]
         top8 = jnp.full((8, QCH), FLOOR, jnp.float32)
         for k in range(bdev // BCH):
@@ -118,57 +141,64 @@
                                 preferred_element_type=jnp.float32)
             for t in range(BCH // TILE):
                 tile = k * (BCH // TILE) + t
-                part = s[t * TILE:(t + 1) * TILE, :] * SCALE2 + bias_scr[tile:tile + 1, cols]
-                s_scr[c % 2, tile * TILE:(tile + 1) * TILE, :] = part
+                bias = jnp.concatenate([bias_scr[c * half + u, tile:tile + 1, :] for u in range(half)], axis=1)
+                part = s[t * TILE:(t + 1) * TILE, :] * SCALE2 + bias
+                s_scr[step % 2, tile * TILE:(tile + 1) * TILE, :] = part
                 top8 = jnp.maximum(top8, jnp.max(part.reshape(TILE // 8, 8, QCH), axis=0))
         top = jnp.max(top8, axis=0, keepdims=True)
         sum8 = jnp.zeros((8, QCH), jnp.float32)
         for tile in range(tiles):
             rows = slice(tile * TILE, (tile + 1) * TILE)
-            p = jnp.exp2(s_scr[c % 2, rows, :] - top)
+            p = jnp.exp2(s_scr[step % 2, rows, :] - top)
             sum8 = sum8 + jnp.sum(p.reshape(TILE // 8, 8, QCH), axis=0)
             p_scr[rows, cols] = p.astype(jnp.bfloat16)
         total = jnp.sum(sum8, axis=0, keepdims=True)
-        for t in range(QCH // TILE):
-            b = c * (QCH // TILE) + t
-            stats_scr[me, b:b + 1, :] = top[:, t * TILE:(t + 1) * TILE]
-            stats_scr[me, 8 + b:9 + b, :] = total[:, t * TILE:(t + 1) * TILE]
-        if c == 0:
+        for u in range(half):
+            b = c * half + u
+            stats_scr[me, pl.ds(b, 1), :] = top[:, u * TILE:(u + 1) * TILE]
+            stats_scr[me, pl.ds(8 + b, 1), :] = total[:, u * TILE:(u + 1) * TILE]
+        if step == 0:
             pl.semaphore_wait(barrier, n)
             keys_copy().start()
-
-    own = pl.ds(pl.multiple_of(me * TILE, TILE), TILE)
-    label_row = labels_ref[pl.ds(me, 1), :]
-    row_ids = lax.broadcasted_iota(jnp.int32, (qdev, TILE), 0)
-
-    def picked(table, start):
-        hot = jnp.where(row_ids + start == label_row, 1.0, 0.0).astype(jnp.bfloat16)
-        return lax.dot_general(hot, table, (((0,), (0,)), ((), ())), preferred_element_type=jnp.float32)
-
-    key_rows = picked(keys_ref[...], mine * qdev)
-    keys_copy().wait()
-    key_rows = key_rows + picked(keys_scr[...], other * qdev)
-    prod = q_ref[own, :].astype(jnp.float32) * key_rows
-    own_pos = jnp.sum(jnp.transpose(prod), axis=0, keepdims=True) / TAU
-    stats_scr[me, 16:24, :] = jnp.broadcast_to(own_pos, (8, TILE))
-
-    def to_peer(d, src, dst, send, recv):
-        return pltpu.make_async_remote_copy(
-            src_ref=src, dst_ref=dst, send_sem=send.at[d], recv_sem=recv.at[d],
-            device_id={"bank": lax.rem(me + d, n)}, device_id_type=MESH)
-
-    stats = [to_peer(d, stats_scr.at[me], stats_scr.at[me], stats_send, stats_recv) for d in range(1, n)]
-    for copy in stats:
-        copy.start()
-
-    for c in range(qdev // QCH):
-        cols = slice(c * QCH, (c + 1) * QCH)
-        neg_scr[:, cols] = jnp.dot(bankt_scr[...], p_scr[:, cols], preferred_element_type=jnp.float32)
+        if step == levels - 1:
+            stats = [to_bank(lax.rem(me + d, n), stats_scr.at[me], stats_scr.at[me], stats_send.at[d], stats_recv.at[d])
+                     for d in range(1, n)]
+            for copy in stats:
+                copy.start()
+        neg = jnp.dot(bankt_scr[...], p_scr[:, cols], preferred_element_type=jnp.float32).astype(jnp.bfloat16)
+        for u in range(half):
+            stage_scr[c * half + u] = neg[:, u * TILE:(u + 1) * TILE]
+        for dx in range(2):
+            if step == levels - 1 and dx == 0:
+                continue
+            j = 2 * step + dx
+            peer = c * half + lax.rem(x + dx, 2)
+            copy = to_bank(peer, stage_scr.at[peer], rs_scr.at[j], rs_send.at[j], rs_recv.at[j])
+            copy.start()
+            scatter.append((j, lax.rem(z + 2 * levels - step - 1, levels) * 2 + lax.rem(x + 2 - dx, 2), copy))
+
+        if step == 1:
+            loads[3].wait()
+            loads[4].wait()
+            own = pl.ds(pl.multiple_of(me * TILE, TILE), TILE)
+            label_row = labels_ref[pl.ds(me, 1), :]
+            row_ids = lax.broadcasted_iota(jnp.int32, (qdev, TILE), 0)
+
+            def picked(table, start):
+                hot = jnp.where(row_ids + start == label_row, 1.0, 0.0).astype(jnp.bfloat16)
+                return lax.dot_general(hot, table, (((0,), (0,)), ((), ())), preferred_element_type=jnp.float32)
+
+            key_rows = picked(keys_ref[...], mine * qdev)
+            keys_copy().wait()
+            key_rows = key_rows + picked(keys_scr[...], other * qdev)
+            prod = q_ref[own, :].astype(jnp.float32) * key_rows
+            own_pos = jnp.sum(jnp.transpose(prod), axis=0, keepdims=True) / TAU
+            stats_scr[me, 16:24, :] = jnp.broadcast_to(own_pos, (8, TILE))
 
     for copy in stats:
         copy.wait()
-    high = jnp.concatenate([stats_scr[b, 16:17, :] for b in range(n)], axis=0) * LOG2E
-    pos = high
+    pos = jnp.concatenate([stats_scr[b, 16:17, :] for b in range(n)], axis=0) * LOG2E
+    high = pos
     for b in range(n):
         high = jnp.maximum(high, stats_scr[b, 0:8, :])
     total = jnp.exp2(pos - high)
@@ -178,13 +208,28 @@
     loss_ref[...] = (lse - pos) * LN2
     alpha = jnp.exp2(stats_scr[me, 0:8, :] - lse)
 
-    for b in range(blocks):
-        stage_scr[b] = (neg_scr[:, b * TILE:(b + 1) * TILE] * alpha[b:b + 1, :]).astype(jnp.bfloat16)
-    scatter = []
-    for d in range(1, n):
-        copy = to_peer(d, stage_scr.at[lax.rem(me + d, n)], rs_scr.at[d], rs_send, rs_recv)
+    row_of = lax.broadcasted_iota(jnp.int32, (n, TILE), 0) == me
+
+    def own_row(rows):
+        return jnp.sum(jnp.where(row_of, rows, 0.0), axis=0, keepdims=True)
+
+    own_lse = own_row(lse)
+    factor = own_row(jnp.exp2(pos - lse) - 1.0)
+    negs = stage_scr[me].astype(jnp.float32) * own_row(alpha)
+    for j, sender, copy in scatter:
+        copy.wait()
+        scale = jnp.exp2(stats_scr[sender, pl.ds(me, 1), :] - own_lse)
+        negs = negs + rs_scr[j].astype(jnp.float32) * scale
+    grad = (jnp.transpose(negs) + wide_column(factor, width) * key_rows) / TAU
+    grad_ref[me] = grad.astype(jnp.bfloat16)
+    along = []
+    for k in range(levels - 1):
+        peer = lax.rem(z + k + 1, levels) * 2 + x
+        along.append(to_bank(peer, grad_ref.at[me], grad_ref.at[me], ag_send.at[k], ag_recv.at[k]))
+    across = z * 2 + 1 - x
+    sides = [to_bank(across, grad_ref.at[me], grad_ref.at[me], ag_send.at[levels - 1], ag_recv.at[levels - 1])]
+    for copy in along + sides:
         copy.start()
-        scatter.append(copy)
 
     for b in range(blocks):
         rows = slice(b * TILE, (b + 1) * TILE)
@@ -200,19 +245,13 @@
         copy.start()
         exchange.append(copy)
 
-    row_of = lax.broadcasted_iota(jnp.int32, (n, TILE), 0) == me
-    factor = jnp.sum(jnp.where(row_of, jnp.exp2(pos - lse) - 1.0, 0.0), axis=0, keepdims=True)
-    negs = stage_scr[me].astype(jnp.float32)
-    for d in range(1, n):
-        scatter[d - 1].wait()
-        negs = negs + rs_scr[d].astype(jnp.float32)
-    grad = (jnp.transpose(negs) + wide_column(factor, width) * key_rows) / TAU
-    grad_ref[me] = grad.astype(jnp.bfloat16)
-    gather = []
-    for d in range(1, n):
-        copy = to_peer(d, grad_ref.at[me], grad_ref.at[me], ag_send, ag_recv)
+    for k in range(levels - 1):
+        along[k].wait_recv()
+        source = lax.rem(z + 2 * levels - k - 1, levels) * 2 + x
+        j = levels + k
+        copy = to_bank(across, grad_ref.at[source], grad_ref.at[source], ag_send.at[j], ag_recv.at[j])
         copy.start()
-        gather.append(copy)
+        sides.append(copy)
 
     for k in range(bdev // BCH):
         rows = slice(k * BCH, (k + 1) * BCH)
@@ -221,7 +260,9 @@
         fresh = bank_ref[rows, :].astype(jnp.float32) + eta * pull
         fresh = fresh * lax.rsqrt(jnp.mean(fresh * fresh, axis=1, keepdims=True) + EPS)
         new_ref[rows, :] = fresh.astype(jnp.bfloat16)
-    for copy in gather:
+    for copy in along:
+        copy.wait_send()
+    for copy in sides:
         copy.wait()
 
 
@@ -231,6 +272,7 @@
     bdev = bank.shape[0]
     eta = 0.25 * (bdev * n) / (qdev * lax.axis_size("batch"))
     vmem = pl.BlockSpec(memory_space=pltpu.VMEM)
+    hbm = pl.BlockSpec(memory_space=pltpu.HBM)
     dma = pltpu.SemaphoreType.DMA
     new_bank, grad, loss = pl.pallas_call(
         functools.partial(step_kernel, n, eta),
@@ -239,14 +281,18 @@
             jax.ShapeDtypeStruct((n, TILE, width), jnp.bfloat16),
             jax.ShapeDtypeStruct((n, TILE), jnp.float32),
         ),
-        in_specs=[pl.BlockSpec(memory_space=pltpu.SMEM)] + [vmem] * 4,
+        in_specs=[hbm] * 5,
         out_specs=(vmem, vmem, vmem),
         scratch_shapes=[
+            pltpu.SMEM(mask_tiles.shape, jnp.int32),
+            pltpu.VMEM((bdev, width), jnp.bfloat16),
+            pltpu.VMEM((qdev, width), jnp.bfloat16),
+            pltpu.VMEM((qdev, width), jnp.bfloat16),
+            pltpu.VMEM((n, TILE), jnp.int32),
             pltpu.VMEM((2, bdev, QCH), jnp.float32),
             pltpu.VMEM((bdev, qdev), jnp.bfloat16),
             pltpu.VMEM((width, bdev), jnp.bfloat16),
-            pltpu.VMEM((bdev // TILE, qdev), jnp.float32),
-            pltpu.VMEM((width, qdev), jnp.float32),
+            pltpu.VMEM((n, bdev // TILE, TILE), jnp.float32),
             pltpu.VMEM((qdev, width), jnp.bfloat16),
             pltpu.VMEM((n, 24, TILE), jnp.float32),
             pltpu.VMEM((qdev, width), jnp.bfloat16),
@@ -254,6 +300,7 @@
             pltpu.VMEM((n, width, TILE), jnp.bfloat16),
             pltpu.VMEM((bdev, width), jnp.bfloat16),
             pltpu.VMEM((bdev, width), jnp.bfloat16),
+            dma((5,)),
             dma((2,)),
             dma((n,)), dma((n,)),
             dma((n,)), dma((n,)),

time: 44.9 us -> 40.9 us (0.911)
  Pallas kernels: 36.6 us -> 32.6 us
    pallas_call x1, Pallas kernels: 36.6 us -> 32.6 us  [fused(): pl.pallas_call(functools.partial(step_kernel, n, eta), out_shape=(jax.Sha...]
where the time goes in v2:
time: 40.9 us; the launch traced here: 40.5 us
  Pallas kernels  32.6 us (80%)
  local copies, waits for them, and re-layouts  6.25 us (15%)
  other arithmetic  1.08 us (3%)
  between operations  0.65 us (2%)
    pallas_call x1, Pallas kernels, fused(): pl.pallas_call(functools.partial(step_kernel, n, eta), out_shape=(jax.Sha...  32.6 us
    unnamed x12, local copies, waits for them, and re-layouts  6.25 us
    convert_element_type x1, other arithmetic, fused(): grad.reshape(qdev, width).astype(jnp.float32)  1.08 us

profile of v2, /device:TPU:0, one launch (start us, length us, event | category | flops | bytes accessed | tf_op | source)
XLA Modules:
  0.0 40.5 jit_solution(11405247734835821739)
XLA Ops:
  0.6 0.0 copy-start
  0.6 1.2 %copy-done = bf16[2048,256]{1,0:T(8,128)(2,1)S(1)} copy-done((bf16[2048,256]{1,0:T(8,128)(2,1)S(1)}, bf16[2048,256]{1,0:T(8,128)(2,1)}, u32[]{:S(2)}) %copy-start) | copy-done | bytes 1048600
  1.9 0.0 copy-start.1
  1.9 1.0 %copy-done.1 = bf16[1024,256]{1,0:T(8,128)(2,1)S(1)} copy-done((bf16[1024,256]{1,0:T(8,128)(2,1)S(1)}, bf16[1024,256]{1,0:T(8,128)(2,1)}, u32[]{:S(2)}) %copy-start.1) | copy-done | bytes 524312
  2.9 0.0 copy-start.2
  2.9 1.0 %copy-done.2 = bf16[1024,256]{1,0:T(8,128)(2,1)S(1)} copy-done((bf16[1024,256]{1,0:T(8,128)(2,1)S(1)}, bf16[1024,256]{1,0:T(8,128)(2,1)}, u32[]{:S(2)}) %copy-start.2) | copy-done | bytes 524312
  3.9 0.0 copy-start.3
  3.9 0.7 %copy-done.3 = s32[16,16]{1,0:T(8,128)S(1)} copy-done((s32[16,16]{1,0:T(8,128)S(1)}, s32[16,16]{1,0:T(8,128)}, u32[]{:S(2)}) %copy-start.3) | copy-done | bytes 1048
  4.6 0.0 copy-start.4
  4.6 0.7 %copy-done.4 = s32[1024]{0:T(1024)S(1)} copy-done((s32[1024]{0:T(1024)S(1)}, s32[1024]{0:T(1024)}, u32[]{:S(2)}) %copy-start.4) | copy-done | bytes 4120
  5.3 32.6 %shard_map.76 = (bf16[2048,256]{1,0:T(8,128)(2,1)S(1)}, bf16[8,128,256]{2,1,0:T(8,128)(2,1)S(1)}, f32[8,128]{1,0:T(8,128)S(1)}) custom-call(s32[16,16]{1,0:T(8,128)S(1)} %copy-done.3, bf16[2048,256]{1,0:T(8,128)(2,1)S(1)} %copy-done, bf16[1024,256]{1,0:T(8,128)(2,1)S(1)} %copy-done.1, bf16[1024,256]{1,0:T(8,128)(2,1)S(1)} %copy-done.2, s32[8,128]{1,0:T(8,128)S(1)} %bitcast.5), custom_call_target="tpu_custom_call" | custom-call | tf_op jit(solution)/shard_map/pallas_call | solution.py:277
  37.9 1.1 %bitcast_convert_fusion = f32[1024,256]{1,0:T(8,128)} fusion(bf16[8,128,256]{2,1,0:T(8,128)(2,1)S(1)} %get-tuple-element.7), kind=kLoop, calls=%fused_computation | loop fusion | flops 262144 | bytes 1572864 | tf_op jit(solution)/shard_map/convert_element_type | solution.py:314
  39.0 1.0 %copy.10 = bf16[2048,256]{1,0:T(8,128)(2,1)} copy(bf16[2048,256]{1,0:T(8,128)(2,1)S(1)} %get-tuple-element.12) | data formatting | bytes 2097152
  40.0 0.6 %copy.11 = f32[1024]{0:T(1024)} copy(f32[1024]{0:T(1024)S(1)} %bitcast.6) | data formatting | bytes 8192
Async XLA Ops:
  0.6 1.2 %copy-start = (bf16[2048,256]{1,0:T(8,128)(2,1)S(1)}, bf16[2048,256]{1,0:T(8,128)(2,1)}, u32[]{:S(2)}) copy-start(bf16[2048,256]{1,0:T(8,128)(2,1)} %bank_hbm.1) | copy-start | bytes 3145732
  1.9 1.0 %copy-start.1 = (bf16[1024,256]{1,0:T(8,128)(2,1)S(1)}, bf16[1024,256]{1,0:T(8,128)(2,1)}, u32[]{:S(2)}) copy-start(bf16[1024,256]{1,0:T(8,128)(2,1)} %q_hbm.1) | copy-start | bytes 1572868
  2.9 1.0 %copy-start.2 = (bf16[1024,256]{1,0:T(8,128)(2,1)S(1)}, bf16[1024,256]{1,0:T(8,128)(2,1)}, u32[]{:S(2)}) copy-start(bf16[1024,256]{1,0:T(8,128)(2,1)} %keys_hbm.1) | copy-start | bytes 1572868
  3.9 0.7 %copy-start.3 = (s32[16,16]{1,0:T(8,128)S(1)}, s32[16,16]{1,0:T(8,128)}, u32[]{:S(2)}) copy-start(s32[16,16]{1,0:T(8,128)} %mask_hbm.1) | copy-start | bytes 3076
  4.6 0.7 %copy-start.4 = (s32[1024]{0:T(1024)S(1)}, s32[1024]{0:T(1024)}, u32[]{:S(2)}) copy-start(s32[1024]{0:T(1024)} %param.8) | copy-start | bytes 12292

commit v3 on v2

--- a/solution.py
+++ b/solution.py
@@ -77,8 +77,8 @@
     new_ref, grad_ref, loss_ref,
     mask_ref, bank_ref, q_ref, keys_ref, labels_ref,
     s_scr, p_scr, bankt_scr, bias_scr, keys_scr, stats_scr, qs_scr,
-    stage_scr, rs_scr, pull_scr, pull_in_scr,
-    in_sems, keys_sems, stats_send, stats_recv, rs_send, rs_recv, ag_send, ag_recv, pull_send, pull_recv,
+    stage_scr, side_scr, top_out_scr, top_in_scr, pair_scr, rs_scr, pull_scr, pull_in_scr,
+    in_sems, keys_sems, stats_send, stats_recv, side_send, side_recv, top_send, top_recv, rs_send, rs_recv, ag_send, ag_recv, pull_send, pull_recv,
 ):
     me = lax.axis_index("bank")
     mine = lax.axis_index("batch")
@@ -130,7 +130,25 @@
             device_id={"bank": peer}, device_id_type=MESH)
 
     half = QCH // TILE
+    across = z * 2 + 1 - x
     scatter = []
+    sides = []
+    kept = []
+
+    def forward(step):
+        for copy in sides[step]:
+            copy.wait()
+        came = top_in_scr[step, 0:1, :]
+        both = jnp.maximum(kept[step], came)
+        pair_scr[step] = (
+            stage_scr[step, x].astype(jnp.float32) * jnp.exp2(kept[step] - both)
+            + side_scr[step].astype(jnp.float32) * jnp.exp2(came - both)
+        ).astype(jnp.bfloat16)
+        copy = to_bank(lax.rem(z + step + 1, levels) * 2 + x, pair_scr.at[step], rs_scr.at[step],
+                       rs_send.at[step], rs_recv.at[step])
+        copy.start()
+        scatter.append(copy)
+
     for step in range(levels):
         c = lax.rem(z + step + 1, levels)
         cols = pl.ds(pl.multiple_of(c * QCH, QCH), QCH)
@@ -167,15 +185,19 @@
                 copy.start()
         neg = jnp.dot(bankt_scr[...], p_scr[:, cols], preferred_element_type=jnp.float32).astype(jnp.bfloat16)
         for u in range(half):
-            stage_scr[c * half + u] = neg[:, u * TILE:(u + 1) * TILE]
-        for dx in range(2):
-            if step == levels - 1 and dx == 0:
-                continue
-            j = 2 * step + dx
-            peer = c * half + lax.rem(x + dx, 2)
-            copy = to_bank(peer, stage_scr.at[peer], rs_scr.at[j], rs_send.at[j], rs_recv.at[j])
+            stage_scr[step, u] = neg[:, u * TILE:(u + 1) * TILE]
+        halves = [top[:, u * TILE:(u + 1) * TILE] for u in range(half)]
+        kept.append(jnp.where(x == 0, halves[0], halves[1]))
+        top_out_scr[step] = jnp.broadcast_to(jnp.where(x == 0, halves[1], halves[0]), (8, TILE))
+        pair = (
+            to_bank(across, stage_scr.at[step, 1 - x], side_scr.at[step], side_send.at[step], side_recv.at[step]),
+            to_bank(across, top_out_scr.at[step], top_in_scr.at[step], top_send.at[step], top_recv.at[step]),
+        )
+        for copy in pair:
             copy.start()
-            scatter.append((j, lax.rem(z + 2 * levels - step - 1, levels) * 2 + lax.rem(x + 2 - dx, 2), copy))
+        sides.append(pair)
+        if step > 0:
+            forward(step - 1)
 
         if step == 1:
             loads[3].wait()
@@ -215,18 +237,23 @@
 
     own_lse = own_row(lse)
     factor = own_row(jnp.exp2(pos - lse) - 1.0)
-    negs = stage_scr[me].astype(jnp.float32) * own_row(alpha)
-    for j, sender, copy in scatter:
+    for copy in sides[levels - 1]:
         copy.wait()
-        scale = jnp.exp2(stats_scr[sender, pl.ds(me, 1), :] - own_lse)
-        negs = negs + rs_scr[j].astype(jnp.float32) * scale
+    negs = (
+        stage_scr[levels - 1, x].astype(jnp.float32) * jnp.exp2(kept[levels - 1] - own_lse)
+        + side_scr[levels - 1].astype(jnp.float32) * jnp.exp2(top_in_scr[levels - 1, 0:1, :] - own_lse)
+    )
+    for step in range(levels - 1):
+        scatter[step].wait()
+        level = lax.rem(z + 2 * levels - step - 1, levels) * 2
+        both = jnp.maximum(stats_scr[level, pl.ds(me, 1), :], stats_scr[level + 1, pl.ds(me, 1), :])
+        negs = negs + rs_scr[step].astype(jnp.float32) * jnp.exp2(both - own_lse)
     grad = (jnp.transpose(negs) + wide_column(factor, width) * key_rows) / TAU
     grad_ref[me] = grad.astype(jnp.bfloat16)
     along = []
     for k in range(levels - 1):
         peer = lax.rem(z + k + 1, levels) * 2 + x
         along.append(to_bank(peer, grad_ref.at[me], grad_ref.at[me], ag_send.at[k], ag_recv.at[k]))
-    across = z * 2 + 1 - x
     sides = [to_bank(across, grad_ref.at[me], grad_ref.at[me], ag_send.at[levels - 1], ag_recv.at[levels - 1])]
     for copy in along + sides:
         copy.start()
@@ -296,19 +323,25 @@
             pltpu.VMEM((qdev, width), jnp.bfloat16),
             pltpu.VMEM((n, 24, TILE), jnp.float32),
             pltpu.VMEM((qdev, width), jnp.bfloat16),
-            pltpu.VMEM((n, width, TILE), jnp.bfloat16),
-            pltpu.VMEM((n, width, TILE), jnp.bfloat16),
+            pltpu.VMEM((n // 2, 2, width, TILE), jnp.bfloat16),
+            pltpu.VMEM((n // 2, width, TILE), jnp.bfloat16),
+            pltpu.VMEM((n // 2, 8, TILE), jnp.float32),
+            pltpu.VMEM((n // 2, 8, TILE), jnp.float32),
+            pltpu.VMEM((n // 2, width, TILE), jnp.bfloat16),
+            pltpu.VMEM((n // 2, width, TILE), jnp.bfloat16),
             pltpu.VMEM((bdev, width), jnp.bfloat16),
             pltpu.VMEM((bdev, width), jnp.bfloat16),
             dma((5,)),
             dma((2,)),
             dma((n,)), dma((n,)),
+            dma((n // 2,)), dma((n // 2,)),
+            dma((n // 2,)), dma((n // 2,)),
             dma((n,)), dma((n,)),
             dma((n,)), dma((n,)),
             dma((bdev // BCH,)), dma((bdev // BCH,)),
         ],
         compiler_params=pltpu.CompilerParams(
-            collective_id=0, has_side_effects=True, vmem_limit_bytes=48 * 1024 * 1024
+            collective_id=0, has_side_effects=True, vmem_limit_bytes=60 * 1024 * 1024
         ),
     )(mask_tiles, bank, queries, keys, labels.reshape(n, TILE))
     return (new_bank, grad.reshape(qdev, width).astype(jnp.float32), loss.reshape(qdev))

time: 40.9 us -> 35.5 us (0.87)
  local copies, waits for them, and re-layouts: 6.25 us -> 1.57 us
  Pallas kernels: 32.6 us -> 30.9 us
  other arithmetic: 1.08 us -> 2.17 us
    unnamed x12 -> x6, local copies, waits for them, and re-layouts: 6.25 us -> 1.57 us
    pallas_call x1, Pallas kernels: 32.6 us -> 30.9 us  [fused(): pl.pallas_call(functools.partial(step_kernel, n, eta), out_shape=(jax.Sha...]
    convert_element_type x1, other arithmetic: 1.08 us -> 2.17 us  [fused(): grad.reshape(qdev, width).astype(jnp.float32)]
where the time goes in v3:
time: 35.5 us; the launch traced here: 35.3 us
  Pallas kernels  30.9 us (87%)
  other arithmetic  2.17 us (6%)
  local copies, waits for them, and re-layouts  1.57 us (4%)
  between operations  0.65 us (2%)
    pallas_call x1, Pallas kernels, fused(): pl.pallas_call(functools.partial(step_kernel, n, eta), out_shape=(jax.Sha...  30.9 us
    convert_element_type x1, other arithmetic, fused(): grad.reshape(qdev, width).astype(jnp.float32)  2.17 us
    unnamed x6, local copies, waits for them, and re-layouts  1.57 us

profile of v3, /device:TPU:0, one launch (start us, length us, event | category | flops | bytes accessed | tf_op | source)
XLA Modules:
  0.0 35.3 jit_solution(404096647994502035)
XLA Ops:
  0.6 30.9 %shard_map.76 = (bf16[2048,256]{1,0:T(8,128)(2,1)}, bf16[8,128,256]{2,1,0:T(8,128)(2,1)}, f32[8,128]{1,0:T(8,128)}) custom-call(s32[16,16]{1,0:T(8,128)} %mask_hbm.1, bf16[2048,256]{1,0:T(8,128)(2,1)} %bank_hbm.1, bf16[1024,256]{1,0:T(8,128)(2,1)} %q_hbm.1, bf16[1024,256]{1,0:T(8,128)(2,1)} %keys_hbm.1, s32[8,128]{1,0:T(8,128)} %bitcast.5), custom_call_target="tpu_custom_call" | custom-call | tf_op jit(solution)/shard_map/pallas_call | solution.py:304
  31.6 0.0 copy-start
  31.6 2.2 %bitcast_convert_fusion = f32[1024,256]{1,0:T(8,128)} fusion(bf16[8,128,256]{2,1,0:T(8,128)(2,1)} %get-tuple-element.7), kind=kLoop, calls=%fused_computation | loop fusion | flops 262144 | bytes 1572864 | tf_op jit(solution)/shard_map/convert_element_type | solution.py:347
  33.8 0.0 copy-done
  33.8 0.0 copy-start.1
  33.8 1.0 %copy.10 = bf16[2048,256]{1,0:T(8,128)(2,1)} copy(bf16[2048,256]{1,0:T(8,128)(2,1)S(1)} %copy-done) | data formatting | bytes 2097152
  34.7 0.0 copy-done.1
  34.7 0.6 %copy.11 = f32[1024]{0:T(1024)} copy(f32[1024]{0:T(1024)S(1)} %bitcast.6) | data formatting | bytes 8192
Async XLA Ops:
  31.6 2.2 %copy-start = (bf16[2048,256]{1,0:T(8,128)(2,1)S(1)}, bf16[2048,256]{1,0:T(8,128)(2,1)}, u32[]{:S(2)}) copy-start(bf16[2048,256]{1,0:T(8,128)(2,1)} %get-tuple-element.12) | copy-start | bytes 3145732
  33.8 1.0 %copy-start.1 = (f32[8,128]{1,0:T(8,128)S(1)}, f32[8,128]{1,0:T(8,128)}, u32[]{:S(2)}) copy-start(f32[8,128]{1,0:T(8,128)} %get-tuple-element.8) | copy-start | bytes 12292

commit v4 on v3

--- a/solution.py
+++ b/solution.py
@@ -344,7 +344,37 @@
             collective_id=0, has_side_effects=True, vmem_limit_bytes=60 * 1024 * 1024
         ),
     )(mask_tiles, bank, queries, keys, labels.reshape(n, TILE))
-    return (new_bank, grad.reshape(qdev, width).astype(jnp.float32), loss.reshape(qdev))
+    new_bank, query_grad, loss = finish(new_bank, grad.reshape(qdev, width), loss)
+    return (new_bank, query_grad, loss.reshape(qdev))
+
+
+def finish_kernel(bank_in, grad_in, loss_in, bank_out, grad_out, loss_out):
+    bank_out[...] = bank_in[...]
+    grad_out[...] = grad_in[...].astype(jnp.float32)
+    loss_out[...] = loss_in[...]
+
+
+def finish(new_bank, grad, loss):
+    bdev, width = new_bank.shape
+    qdev = grad.shape[0]
+    steps = 2
+    whole = pl.BlockSpec(loss.shape, lambda i: (0, 0))
+    specs = (
+        pl.BlockSpec((bdev // steps, width), lambda i: (i, 0)),
+        pl.BlockSpec((qdev // steps, width), lambda i: (i, 0)),
+        whole,
+    )
+    return pl.pallas_call(
+        finish_kernel,
+        grid=(steps,),
+        out_shape=(
+            jax.ShapeDtypeStruct((bdev, width), jnp.bfloat16),
+            jax.ShapeDtypeStruct((qdev, width), jnp.float32),
+            jax.ShapeDtypeStruct(loss.shape, jnp.float32),
+        ),
+        in_specs=list(specs),
+        out_specs=specs,
+    )(new_bank, grad, loss)
 
 
 def on_device(bank, queries, keys, labels, mask_tiles):

time: 35.5 us -> 34.3 us (0.966)
  Pallas kernels: 30.9 us -> 33.4 us
  other arithmetic: 2.17 us -> 0 us
  local copies, waits for them, and re-layouts: 1.57 us -> 0 us
    pallas_call x0 -> x1, Pallas kernels: none -> 2.5 us  [finish(): pl.pallas_call(finish_kernel, grid=(steps,), out_shape=(jax.ShapeDtypeStr...]
    convert_element_type x1 -> x0, other arithmetic: 2.17 us -> none  [fused(): grad.reshape(qdev, width).astype(jnp.float32)]
    unnamed x6 -> x0, local copies, waits for them, and re-layouts: 1.57 us -> none
where the time goes in v4:
time: 34.3 us; the launch traced here: 34.1 us
  Pallas kernels  33.4 us (97%)
  between operations  0.64 us (2%)
    pallas_call x1, Pallas kernels, fused(): pl.pallas_call(functools.partial(step_kernel, n, eta), out_shape=(jax.Sha...  30.9 us
    pallas_call x1, Pallas kernels, finish(): pl.pallas_call(finish_kernel, grid=(steps,), out_shape=(jax.ShapeDtypeStr...  2.5 us

profile of v4, /device:TPU:0, one launch (start us, length us, event | category | flops | bytes accessed | tf_op | source)
XLA Modules:
  0.0 34.1 jit_solution(3569198636141103386)
XLA Ops:
  0.6 30.9 %shard_map.76 = (bf16[2048,256]{1,0:T(8,128)(2,1)}, bf16[8,128,256]{2,1,0:T(8,128)(2,1)}, f32[8,128]{1,0:T(8,128)}) custom-call(s32[16,16]{1,0:T(8,128)} %mask_hbm.1, bf16[2048,256]{1,0:T(8,128)(2,1)} %bank_hbm.1, bf16[1024,256]{1,0:T(8,128)(2,1)} %q_hbm.1, bf16[1024,256]{1,0:T(8,128)(2,1)} %keys_hbm.1, s32[8,128]{1,0:T(8,128)} %bitcast.4), custom_call_target="tpu_custom_call" | custom-call | tf_op jit(solution)/shard_map/pallas_call | solution.py:304
  31.6 2.5 %shard_map.77 = (bf16[2048,256]{1,0:T(8,128)(2,1)}, f32[1024,256]{1,0:T(8,128)}, f32[8,128]{1,0:T(8,128)}) custom-call(bf16[2048,256]{1,0:T(8,128)(2,1)} %get-tuple-element.9.bank_in, bf16[1024,256]{1,0:T(8,128)(2,1)} %bitcast.3, f32[8,128]{1,0:T(8,128)} %get-tuple-element.11.loss_in), custom_call_target="tpu_custom_call" | custom-call | tf_op jit(solution)/shard_map/pallas_call | solution.py:367
